TPU v7x, 32 devices: a whole 2x2x4 slice. The times are simulated.
32 devices in a mesh: parts: 2 (over x), chan: 4 (over y, core), tmpl: 4 (over z).
Axes of the slice: x: 2, y: 2, z: 4, core: 2. Of those that a mesh axis runs over, the one named last changes fastest.
Arguments:
- raw_traces: float32 [4096, 2816], P(('chan', 'tmpl'), 'parts'), parts along dimension 1, may hold values from -50 to 50
- filter_taps: float32 [129], replicated, may hold values from -0.5 to 0.5
- templates: bfloat16 [32, 200, 4096], P('tmpl', None, 'chan'), may hold values from -6 to 6
- offsets: int32 [32], P('tmpl'), may hold values from 0 to 56
- channel_mask: int32 [32, 4096], P('tmpl'), may hold values from 0 to 1, as said below
Outputs:
- detection: float32 [32, 2048], P('tmpl', ('parts', 'chan')), parts along dimension 1
There are 2 independent parts, one for each index of `parts`. A program takes and returns all parts, laid end to end along the dimension named above; an argument that names none is the same for every part. Nothing has to cross between parts.
Inputs may be any that keep to these rules, and one draw needn't show every extreme that they name: `channel_mask`: each template uses one contiguous run of 4 or more blocks of 128 channels, starting and ending at multiples of 128; some template uses all channels.
All inputs are finite; a program needn't handle non-finite values.
Results may differ from a plain program's by a relative error of at most 0.004.
Values may be sent and summed in bfloat16 or wider, within the bound.
A program may use at most 128 MiB of HBM per device.

v0:
```python
import jax
import jax.numpy as jnp
from jax import lax
from jax.sharding import PartitionSpec as P

CHANNELS = 4096
TMPL_LEN = 200
SPAN = 256
LAG_DEV = 256


def filter_traces(raw_traces, filter_taps):
    block_width = 128
    tap_count = filter_taps.shape[0]
    row_count, length = raw_traces.shape
    out_len = length - tap_count + 1
    block_count = -(-out_len // block_width)
    pieces = raw_traces.reshape(row_count, block_count + 1, block_width)
    spread = jnp.concatenate(
        [filter_taps, jnp.zeros((2 * block_width + 1 - tap_count,), filter_taps.dtype)]
    )
    toeplitz = (
        jnp.tile(spread, block_width)[: 2 * block_width * block_width]
        .reshape(block_width, 2 * block_width)
        .T
    )
    lower = pieces[:, :block_count].reshape(-1, block_width)
    upper = pieces[:, 1:].reshape(-1, block_width)
    output = jnp.dot(
        lower,
        toeplitz[:block_width],
        precision=lax.Precision.HIGHEST,
        preferred_element_type=jnp.float32,
    )
    output = output + jnp.dot(
        upper,
        toeplitz[block_width:],
        precision=lax.Precision.HIGHEST,
        preferred_element_type=jnp.float32,
    )
    output = output.reshape(row_count, block_count * block_width)
    return output.astype(jnp.bfloat16)


def shape_templates(templates, channel_mask):
    values = templates.astype(jnp.float32)
    rms_scale = jnp.sqrt(jnp.mean(values * values, axis=1, keepdims=True) + 1e-06)
    return (channel_mask.astype(jnp.float32)[:, None, :] * values / rms_scale).astype(jnp.bfloat16)


def skew_sum(product, count_out):
    height, length = product.shape
    flattened = jnp.concatenate([product.reshape(-1), jnp.zeros((height,), product.dtype)])
    return flattened.reshape(height, length + 1)[:, :count_out].sum(axis=0)


def shifted_skew(product, offset_value, count_out):
    window = lax.dynamic_slice_in_dim(product, offset_value, count_out + product.shape[0] - 1, 1)
    return skew_sum(window, count_out)


def window_energy(masses, offsets, count_out):

    def one_row(row_values, offset_value):
        return lax.dynamic_slice_in_dim(row_values, offset_value, count_out + TMPL_LEN - 1)

    segments = jax.vmap(one_row)(masses, offsets)
    return lax.reduce_window(
        segments, jnp.zeros((), segments.dtype), lax.add, (1, TMPL_LEN), (1, 1), "VALID"
    )


def unit_masses(mask_rows, trace_rows):
    unit_width = CHANNELS // 32
    unit_count = trace_rows.shape[0] // unit_width
    squares = trace_rows.astype(jnp.float32) ** 2
    unit_sums = squares.reshape(unit_count, unit_width, trace_rows.shape[1]).sum(axis=1)
    unit_flags = mask_rows[:, ::unit_width].astype(jnp.float32)
    return jnp.sum(unit_flags[:, :, None] * unit_sums[None, :, :], axis=1)


def shards(raw_traces, filter_taps, templates, offsets, channel_mask):
    chan_count = lax.axis_size("chan")
    group_size = templates.shape[0]
    tmpl_rows = templates.shape[1]
    local_chans = templates.shape[2]
    window_len = LAG_DEV + SPAN
    filtered = filter_traces(raw_traces, filter_taps)
    first_chan = lax.axis_index("chan") * local_chans
    local_mask = lax.dynamic_slice_in_dim(channel_mask, first_chan, local_chans, 1)
    shaped = shape_templates(templates, local_mask)
    starts = jnp.arange(chan_count, dtype=jnp.int32) * LAG_DEV
    windows = jax.vmap(
        lambda begin_at: lax.dynamic_slice_in_dim(filtered, begin_at, window_len, 1)
    )(starts)
    arrived = lax.all_to_all(windows, "chan", split_axis=0, concat_axis=0, tiled=True)
    gathered = lax.all_gather(arrived, "tmpl", axis=1, tiled=True)
    traces = gathered.reshape(-1, window_len)
    weights = lax.all_gather(shaped, "chan", axis=2, tiled=True)
    count_chans = weights.shape[2]
    stacked = weights.reshape(group_size * tmpl_rows, count_chans)
    product = jnp.dot(stacked, traces, preferred_element_type=jnp.float32)
    totals = product.reshape(group_size, tmpl_rows, window_len)
    numerator = jax.vmap(
        lambda block_rows, offset_value: shifted_skew(block_rows, offset_value, LAG_DEV)
    )(totals, offsets)
    masses = unit_masses(channel_mask, traces)
    energy = window_energy(masses, offsets, LAG_DEV)
    return numerator / jnp.sqrt(energy)


def solution(mesh):
    placed = (
        P(("chan", "tmpl"), "parts"),
        P(),
        P("tmpl", None, "chan"),
        P("tmpl"),
        P("tmpl", None),
    )
    return jax.shard_map(
        shards, mesh=mesh, in_specs=placed, out_specs=P("tmpl", ("parts", "chan")), check_vma=False
    )
```

profile of v0, /device:TPU:0, one launch (start us, length us, event | category | flops | bytes accessed | tf_op | source)
XLA Modules:
  0.0 264.0 jit_solution(6753833753330003833)
XLA Ops:
  6.5 1.8 copy.13
  9.7 2.1 copy.14
  14.7 2.6 fusion.6
  18.9 1.6 convert_element_type.31
  20.5 12.5 %while.2 = (s32[]{:T(128)}, bf16[256,1280]{1,0:T(8,128)(2,1)}, s32[4,2]{0,1:T(2,128)S(1)}, bf16[4,256,512]{2,1,0:T(8,128)(2,1)}, s32[]{:T(128)}) while((s32[]{:T(128)}, bf16[256,1280]{1,0:T(8,128)(2,1)}, s32[4,2]{0,1:T(2,128)S(1)}, bf16[4,256,512]{2,1,0:T(8,128)(2,1)}, s32[]{:T(128)}) %tuple.31), condition=%wide.while_cond, body=%wide.while_body.sunk | while | flops 2 | bytes 525401 | solution.py:94
  21.1 2.8 %bitcast_dynamic-update-slice_fusion.2 = bf16[4,256,512]{2,1,0:T(8,128)(2,1)} fusion(bf16[4,256,512]{2,1,0:T(8,128)(2,1)} %get-tuple-element.103, s32[]{:T(128)} %get-tuple-element.100, bf16[256,1280]{1,0:T(8,128)(2,1)} %get-tuple-element.106, s32[]{:T(128)} %bitcast.28), kind=kLoop, calls=%fused_computation.1.clone.1 | loop fusion | bytes 525312 | tf_op jit(solution)/shard_map/vmap()/gather
  24.5 2.4 bitcast_dynamic-update-slice_fusion.2
  27.5 2.5 bitcast_dynamic-update-slice_fusion.2
  30.6 2.4 bitcast_dynamic-update-slice_fusion.2
  33.0 19.4 %all_to_all.5 = bf16[4,256,512]{2,1,0:T(8,128)(2,1)} all-to-all(bf16[4,256,512]{2,1,0:T(8,128)(2,1)} %get-tuple-element.12), channel_id=1, replica_groups=mesh['parts'=2,'chan'=4,'tmpl'=4] {'chan'}, dimensions={0} | all-to-all | bytes 2097152 | tf_op jit(solution)/shard_map/all_to_all | solution.py:96
  54.1 2.7 %fusion.1 = bf16[8,200,1024]{2,1,0:T(8,128)(2,1)} fusion(bf16[8,200,1024]{2,1,0:T(8,128)(2,1)S(1)} %copy-done, f32[8,1024]{1,0:T(8,128)S(1)} %add_sqrt_fusion, f32[8,1024]{1,0:T(8,128)S(1)} %dynamic-slice_convert_fusion), kind=kLoop, calls=%fused_computation.8 | loop fusion | flops 6553600 | bytes 6619136 | tf_op jit(solution)/shard_map/convert_element_type | solution.py:48
  57.9 76.6 %all-gather.5.cloned.1.call-done = bf16[4,1024,512]{2,1,0:T(8,128)(2,1)} async-done(((bf16[4,256,512]{2,1,0:T(8,128)(2,1)}), bf16[4,1024,512]{2,1,0:T(8,128)(2,1)}) %all-gather.5.cloned.1.call-update) | async-done | bytes 4194320 | tf_op jit(solution)/shard_map/all_gather | solution.py:97
  134.5 6.8 %convert_multiply_fusion = f32[4,1024,512]{2,1,0:T(8,128)} fusion(bf16[4,1024,512]{2,1,0:T(8,128)(2,1)} %all-gather.5.cloned.1.call-done), kind=kLoop, calls=%fused_computation.4 | loop fusion | flops 4194304 | bytes 12582912 | tf_op jit(solution)/shard_map/integer_pow | solution.py:76
  141.2 6.0 %reduce_sum.38 = f32[32,512]{1,0:T(8,128)S(1)} reduce(f32[32,128,512]{2,1,0:T(8,128)} %bitcast.31, f32[]{:T(128)} %constant.3.clone.1), dimensions={1}, to_apply=%region_2.0 | reduce | flops 2080768 | bytes 8454148 | tf_op jit(solution)/shard_map/reduce_sum | solution.py:77
  147.4 15.7 %while.3 = (s32[]{:T(128)}, f32[8,512]{1,0:T(8,128)S(1)}, s32[8,2]{0,1:T(2,128)S(1)}, f32[8,455]{1,0:T(8,128)S(1)}, s32[]{:T(128)}, /*index=5*/s32[]{:T(128)}) while((s32[]{:T(128)}, f32[8,512]{1,0:T(8,128)S(1)}, s32[8,2]{0,1:T(2,128)S(1)}, f32[8,455]{1,0:T(8,128)S(1)}, s32[]{:T(128)}, /*index=5*/s32[]{:T(128)}) %tuple.34), condition=%wide.while_cond.1, body=%wide.while_body.1.sunk | while | flops 2 | bytes 7393 | solution.py:65
  163.1 6.9 %reduce_window.7 = f32[8,256]{1,0:T(8,128)S(1)} reduce-window(f32[8,455]{1,0:T(8,128)S(1)} %get-tuple-element.20, f32[]{:T(128)} %constant.3.clone.1), window={size=1x200}, to_apply=%region_4.0 | reduce-window | flops 407552 | bytes 22756 | tf_op jit(solution)/shard_map/reduce_window | solution.py:68
  170.1 49.5 %all-gather.3.cloned.1.call-done = bf16[8,200,4096]{2,1,0:T(8,128)(2,1)} async-done(((bf16[8,200,1024]{2,1,0:T(8,128)(2,1)}), bf16[8,200,4096]{2,1,0:T(8,128)(2,1)}) %all-gather.3.cloned.1.call-update) | async-done | bytes 13107216 | tf_op jit(solution)/shard_map/all_gather | solution.py:99
  219.6 11.2 %fusion.11 = f32[8,200,512]{2,1,0:T(8,128)S(1)} fusion(bf16[8,200,4096]{2,1,0:T(8,128)(2,1)} %all-gather.3.cloned.1.call-done, bf16[4096,512,1]{1,0,2:T(8,128)(2,1)} %bitcast.33), kind=kOutput, calls=%fused_computation.28 | convolution fusion | flops 6710886400 | bytes 20578304 | tf_op jit(solution)/shard_map/dot_general | solution.py:102
  230.8 3.6 %copy.17 = f32[8,200,512]{1,0,2:T(8,128)} copy(f32[8,200,512]{2,1,0:T(8,128)S(1)} %fusion.11) | data formatting | bytes 6553600 | tf_op jit(solution)/shard_map/dot_general | solution.py:102
  234.4 7.0 %gather_fusion = f32[8,200,455]{1,0,2:T(8,128)} fusion(f32[8,200,512]{1,0,2:T(8,128)} %copy.17, s32[8]{0:T(128)S(1)} %or_bitcast_fusion), kind=kCustom, calls=%fused_computation | custom fusion | bytes 5824096 | tf_op jit(solution)/shard_map/vmap()/gather | solution.py:58
  241.3 3.6 %copy.18 = f32[8,200,455]{2,1,0:T(8,128)S(1)} copy(f32[8,200,455]{1,0,2:T(8,128)} %gather_fusion) | data formatting | bytes 5824000 | tf_op jit(solution)/shard_map/vmap()/gather | solution.py:58
  244.9 3.2 %reshape.64 = f32[8,91000]{1,0:T(8,128)} reshape(f32[8,200,455]{2,1,0:T(8,128)S(1)} %copy.18) | data formatting | bytes 5824000 | tf_op jit(solution)/shard_map/vmap()/reshape | solution.py:53
  248.1 2.0 concatenate.15
  250.1 4.9 %reshape.65 = f32[8,200,456]{2,1,0:T(8,128)} reshape(f32[8,91200]{1,0:T(8,128)S(1)} %concatenate.15) | data formatting | bytes 5836800 | tf_op jit(solution)/shard_map/vmap()/reshape | solution.py:54
  (77 shorter events, 28.5 us)
Async XLA Ops:
  6.5 127.9 %all-gather.5.cloned.1.call-start = ((), (), s32[]{:S(2)}) async-start(), calls=%async_computation.2 | async-start | bytes 5242880 | tf_op jit(solution)/shard_map/all_gather | solution.py:97
  9.7 3.3 %copy-start.1 = (f32[129]{0:T(256)S(1)}, f32[129]{0:T(256)}, u32[]{:S(2)}) copy-start(f32[129]{0:T(256)} %param.6) | copy-start | bytes 1552
  20.5 32.8 %copy-start = (bf16[8,200,1024]{2,1,0:T(8,128)(2,1)S(1)}, bf16[8,200,1024]{2,1,0:T(8,128)(2,1)}, u32[]{:S(2)}) copy-start(bf16[8,200,1024]{2,1,0:T(8,128)(2,1)} %param.7) | copy-start | bytes 9830404
  52.5 167.1 %all-gather.3.cloned.1.call-start = ((), (), s32[]{:S(2)}) async-start(), calls=%async_computation.1 | async-start | bytes 16384000 | tf_op jit(solution)/shard_map/all_gather | solution.py:99
  56.8 1.1 copy-start.2
Sparse Core Ops, SparseCore 0:
  52.6 81.8 all-gather.4
  136.0 83.5 all-gather.2
where the time goes:
time: 265 us; the launch traced here: 264 us
  waiting for transfers between devices  126 us (48%)
  local copies, waits for them, and re-layouts  63.1 us (24%)
  other arithmetic  26.3 us (10%)
  blocking collectives  19.4 us (7%)
  matrix products  15 us (6%)
  between operations  13.6 us (5%)
    all_gather x1, waiting for transfers between devices, shards(): gathered = lax.all_gather(arrived, 'tmpl', axis=1, tiled=True)  76.6 us
    all_gather x1, waiting for transfers between devices, shards(): weights = lax.all_gather(shaped, 'chan', axis=2, tiled=True)  49.5 us
    gather x44, local copies, waits for them, and re-layouts  27.8 us
    all_to_all x1, blocking collectives, shards(): lax.all_to_all(windows, 'chan', split_axis=0, concat_axis=0, tiled=True)  19.4 us
    dot_general x1, matrix products, shards(): product = jnp.dot(stacked, traces, preferred_element_type=jnp.float32)  11.2 us
    gather x2, local copies, waits for them, and re-layouts, shifted_skew(): lax.dynamic_slice_in_dim(product, offset_value, count_out + product.shape...  10.5 us
    another operation x1, other arithmetic, window_energy(): lax.reduce_window(segments, jnp.zeros((), segments.dtype), lax.add, (1, T...  6.92 us
    integer_pow x1, other arithmetic, unit_masses(): squares = trace_rows.astype(jnp.float32) ** 2  6.78 us
  transfers between devices with their start and end apart: 2, of which 2 were waited for; matrix products, arithmetic and copies ran while one was open for 15% of the time, Pallas kernels for 0%

commit v1 on v0

v1 whole, which is shorter than its diff:
```python
import functools

import jax
import jax.numpy as jnp
from jax import lax
from jax.experimental import pallas as pl
from jax.experimental.pallas import tpu as pltpu
from jax.sharding import PartitionSpec as P

SPAN = 256
BLK = 256
LANE = 128
MESH = pl.DeviceIdType.MESH


def left(x, count):
    size = x.shape[-1]
    count = count % size
    return x if count == 0 else pltpu.roll(x, size - count, x.ndim - 1)


def kernel(
    ntm, nch, raw_hbm, taps_ref, tmpl_hbm, mask_hbm, offs_ref, out_ref,
    raw, tap_row, tmpl, mask, skewed, shaped, rall, prod, qacc, units, num_out, en_out,
    num_in, en_in, load_sem, recv_sem, right_sem, left_sem, unit_send, unit_recv,
    num_send, num_recv, en_send, en_recv,
):
    z = lax.axis_index("tmpl")
    c = lax.axis_index("chan")
    rows = raw.shape[0]
    group, tlen, local = tmpl.shape
    nblk = rall.shape[0]
    total = nblk * BLK
    unit = min(LANE, rows)
    nun = rows // unit

    loads = [
        pltpu.make_async_copy(raw_hbm, raw, load_sem.at[0]),
        pltpu.make_async_copy(tmpl_hbm, tmpl, load_sem.at[1]),
        pltpu.make_async_copy(
            mask_hbm.at[:, pl.ds(pl.multiple_of(c * local, LANE), local)], mask, load_sem.at[2]
        ),
    ]
    for item in loads:
        item.start()

    barrier = pltpu.get_barrier_semaphore()
    for d in range(1, ntm):
        pl.semaphore_signal(
            barrier, inc=1, device_id={"tmpl": lax.rem(z + d, ntm)}, device_id_type=MESH
        )
    for d in range(1, nch):
        pl.semaphore_signal(
            barrier, inc=1, device_id={"chan": lax.rem(c + d, nch)}, device_id_type=MESH
        )

    tap_row[...] = jnp.zeros_like(tap_row)
    tap_row[:, : taps_ref.shape[1]] = taps_ref[...]
    band = pltpu.roll(
        jnp.broadcast_to(tap_row[...], (LANE, 2 * LANE)), 0, 1, stride=1, stride_axis=0
    )
    band_hi = band.astype(jnp.bfloat16)
    band_lo = (band - band_hi.astype(jnp.float32)).astype(jnp.bfloat16)
    qacc[...] = jnp.zeros_like(qacc)
    loads[0].wait()
    pl.semaphore_wait(barrier, ntm - 1 + nch - 1)

    def chunk(src, n):
        return rall.at[n, pl.ds(pl.multiple_of(src * rows, rows), rows), :]

    def hop(src, n, sems, step):
        return pltpu.make_async_remote_copy(
            src_ref=chunk(src, n),
            dst_ref=chunk(src, n),
            send_sem=sems.at[src, n],
            recv_sem=recv_sem.at[src, n],
            device_id={"tmpl": lax.rem(z + step + ntm, ntm)},
            device_id_type=MESH,
        )

    def contract(a, b):
        return lax.dot_general(
            a, b, (((1,), (1,)), ((), ())), preferred_element_type=jnp.float32
        )

    def fir(n, carry):
        x = raw[:, pl.ds(pl.multiple_of(n * BLK, BLK), BLK + LANE)]
        hi = x.astype(jnp.bfloat16)
        lo = (x - hi.astype(jnp.float32)).astype(jnp.bfloat16)
        for half in range(BLK // LANE):
            a = hi[:, half * LANE : half * LANE + 2 * LANE]
            b = lo[:, half * LANE : half * LANE + 2 * LANE]
            y = contract(a, band_hi) + (contract(b, band_hi) + contract(a, band_lo))
            y = y.astype(jnp.bfloat16)
            rall[
                n, pl.ds(pl.multiple_of(z * rows, rows), rows), half * LANE : half * LANE + LANE
            ] = y
            y = y.astype(jnp.float32)
            y = y * y
            at = pl.ds(pl.multiple_of(n * BLK + half * LANE, LANE), LANE)
            for u in range(nun):
                units[z, u : u + 1, at] = jnp.sum(
                    y[u * unit : (u + 1) * unit], axis=0, keepdims=True
                )

        @pl.when(z < ntm - 1)
        def _():
            hop(z, n, right_sem, 1).start()

        @pl.when(z > 0)
        def _():
            hop(z, n, left_sem, -1).start()

        return carry

    lax.fori_loop(0, nblk, fir, 0)

    def unit_copy(src, d):
        return pltpu.make_async_remote_copy(
            src_ref=units.at[src],
            dst_ref=units.at[src],
            send_sem=unit_send.at[d],
            recv_sem=unit_recv.at[d],
            device_id={"tmpl": lax.rem(z + d, ntm)},
            device_id_type=MESH,
        )

    for d in range(1, ntm):
        unit_copy(z, d).start()

    loads[1].wait()
    loads[2].wait()

    def shape_cols(i, carry):
        cols = pl.ds(pl.multiple_of(i * LANE, LANE), LANE)
        flags = mask[:, cols].astype(jnp.float32)
        for k in range(group):
            v = tmpl[k, :, cols].astype(jnp.float32)
            power = jnp.mean(v * v, axis=0, keepdims=True)
            scale = flags[k : k + 1, :] / jnp.sqrt(power + 1e-06)
            skewed[pl.ds(k, tlen, stride=group), :] = v * scale
        shaped[:, cols] = skewed[...].astype(jnp.bfloat16)
        return carry

    lax.fori_loop(0, local // LANE, shape_cols, 0)

    offs = jnp.zeros((group, 1), jnp.int32)
    index = lax.broadcasted_iota(jnp.int32, (group, 1), 0)
    for k in range(group):
        offs = jnp.where(index == k, offs_ref[k], offs)

    def shift_rows(x):
        amount = jnp.broadcast_to(offs, x.shape)
        bit = 1
        while bit < SPAN - tlen + 1:
            x = jnp.where((amount & bit) != 0, left(x, bit), x)
            bit *= 2
        return x

    def spread(x, own_ref, in_ref, send, recv):
        lag = own_ref.shape[2]
        for j in range(nch):
            own_ref[j] = x[:, j * lag : (j + 1) * lag]
        for d in range(1, nch):
            other = lax.rem(c + d, nch)
            pltpu.make_async_remote_copy(
                src_ref=own_ref.at[other],
                dst_ref=in_ref.at[d],
                send_sem=send.at[d],
                recv_sem=recv.at[d],
                device_id={"chan": other},
                device_id_type=MESH,
            ).start()

    def collect(own_ref, in_ref, send, recv):
        value = own_ref[c]
        for d in range(1, nch):
            pltpu.make_async_remote_copy(
                src_ref=own_ref.at[lax.rem(c + d, nch)],
                dst_ref=in_ref.at[d],
                send_sem=send.at[d],
                recv_sem=recv.at[d],
                device_id={"chan": lax.rem(c + d, nch)},
                device_id_type=MESH,
            ).wait()
            value = value + in_ref[d]
        return value

    for d in range(1, ntm):
        unit_copy(lax.rem(z + ntm - d, ntm), d).wait()
    masses = jnp.zeros((group, total), jnp.float32)
    for s in range(ntm):
        for u in range(nun):
            at = s * rows + u * unit
            flag = mask[:, at : at + 1].astype(jnp.float32)
            masses = masses + flag * units[s, u : u + 1, :]
    window, width, place, energy = masses, 1, 0, None
    while width <= tlen:
        if tlen & width:
            piece = left(window, place)
            energy = piece if energy is None else energy + piece
            place += width
        window = window + left(window, width)
        width *= 2
    spread(shift_rows(energy), en_out, en_in, en_send, en_recv)

    def arrive(d, n):
        @pl.when(z - d >= 0)
        def _():
            src = lax.rem(z - d + ntm, ntm)
            hop(src, n, right_sem, 1).wait_recv()

            @pl.when(z < ntm - 1)
            def _():
                hop(src, n, right_sem, 1).start()

        @pl.when(z + d < ntm)
        def _():
            src = lax.rem(z + d, ntm)
            hop(src, n, left_sem, -1).wait_recv()

            @pl.when(z > 0)
            def _():
                hop(src, n, left_sem, -1).start()

    def block(n, carry):
        arrive(ntm - 1, n)
        prod[...] = jnp.dot(shaped[...], rall[n], preferred_element_type=jnp.float32)
        blank = jnp.zeros((group, LANE), jnp.float32)
        total_acc = jnp.zeros((group, 2 * BLK), jnp.float32)
        for g in range(min(LANE, tlen)):
            low = prod[group * g : group * (g + 1), :]
            first, second = low[:, :LANE], low[:, LANE:]
            carry_in = blank
            if g + LANE < tlen:
                high = prod[group * (g + LANE) : group * (g + LANE + 1), :]
                carry_in = high[:, :LANE]
                first = first + high[:, LANE:]
            wide = jnp.concatenate([blank, carry_in, first, second], axis=1)
            total_acc = total_acc + left(wide, g)
        at = pl.ds(pl.multiple_of(n * BLK, BLK), 2 * BLK)
        qacc[:, at] = qacc[:, at] + total_acc
        return carry

    def step(d):
        def body(n, carry):
            arrive(d, n)
            return carry

        lax.fori_loop(0, nblk, body, 0)

    for d in range(1, ntm - 1):
        step(d)
    lax.fori_loop(0, nblk, block, 0)

    spread(shift_rows(qacc[:, BLK:]), num_out, num_in, num_send, num_recv)
    energy = collect(en_out, en_in, en_send, en_recv)
    numerator = collect(num_out, num_in, num_send, num_recv)
    out_ref[...] = numerator / jnp.sqrt(energy)

    def drain(n, carry):
        for s in range(ntm):
            @pl.when((s <= z) & (z < ntm - 1))
            def _():
                hop(s, n, right_sem, 1).wait_send()

            @pl.when((s >= z) & (z > 0))
            def _():
                hop(s, n, left_sem, -1).wait_send()

        return carry

    lax.fori_loop(0, nblk, drain, 0)


def shards(raw_traces, filter_taps, templates, offsets, channel_mask):
    ntm = lax.axis_size("tmpl")
    nch = lax.axis_size("chan")
    rows, length = raw_traces.shape
    group, tlen, local = templates.shape
    nblk = (length - filter_taps.shape[0] + 1) // BLK
    total = nblk * BLK
    lag = (total - SPAN) // nch
    nun = rows // min(LANE, rows)
    f32, bf16, dma = jnp.float32, jnp.bfloat16, pltpu.SemaphoreType.DMA
    any_spec = pl.BlockSpec(memory_space=pl.ANY)
    vmem_spec = pl.BlockSpec(memory_space=pltpu.VMEM)
    return pl.pallas_call(
        functools.partial(kernel, ntm, nch),
        out_shape=jax.ShapeDtypeStruct((group, lag), f32),
        in_specs=[
            any_spec, vmem_spec, any_spec, any_spec, pl.BlockSpec(memory_space=pltpu.SMEM),
        ],
        out_specs=vmem_spec,
        scratch_shapes=[
            pltpu.VMEM((rows, length), f32),
            pltpu.VMEM((1, 2 * LANE), f32),
            pltpu.VMEM((group, tlen, local), bf16),
            pltpu.VMEM((group, local), jnp.int32),
            pltpu.VMEM((group * tlen, LANE), f32),
            pltpu.VMEM((group * tlen, local), bf16),
            pltpu.VMEM((nblk, local, BLK), bf16),
            pltpu.VMEM((group * tlen, BLK), f32),
            pltpu.VMEM((group, BLK + total), f32),
            pltpu.VMEM((ntm, nun, total), f32),
            pltpu.VMEM((nch, group, lag), f32),
            pltpu.VMEM((nch, group, lag), f32),
            pltpu.VMEM((nch, group, lag), f32),
            pltpu.VMEM((nch, group, lag), f32),
            dma((3,)),
            dma((ntm, nblk)),
            dma((ntm, nblk)),
            dma((ntm, nblk)),
            dma((ntm,)),
            dma((ntm,)),
            dma((nch,)),
            dma((nch,)),
            dma((nch,)),
            dma((nch,)),
        ],
        compiler_params=pltpu.CompilerParams(
            collective_id=0, has_side_effects=True, vmem_limit_bytes=48 * 1024 * 1024
        ),
    )(raw_traces, filter_taps.reshape(1, -1), templates, channel_mask, offsets)


def solution(mesh):
    placed = (
        P(("chan", "tmpl"), "parts"),
        P(),
        P("tmpl", None, "chan"),
        P("tmpl"),
        P("tmpl", None),
    )
    return jax.shard_map(
        shards, mesh=mesh, in_specs=placed, out_specs=P("tmpl", ("parts", "chan")), check_vma=False
    )
```

time: 265 us -> 64.6 us (0.24)
  waiting for transfers between devices: 126 us -> 0 us
  Pallas kernels: 0 us -> 58.2 us
  local copies, waits for them, and re-layouts: 63.1 us -> 6.13 us
  other arithmetic: 26.3 us -> 0 us
  blocking collectives: 19.4 us -> 0 us
  matrix products: 15 us -> 0 us
  between operations: 13.6 us -> 0.01 us
    all_gather x2 -> x0, waiting for transfers between devices: 126 us -> none  [the longest x1 76.6 us: shards(): gathered = lax.all_gather(arrived, 'tmpl', axis=1, tiled=True)]
    pallas_call x0 -> x1, Pallas kernels: none -> 58.2 us  [shards(): pl.pallas_call(functools.partial(kernel, ntm, nch), out_shape=jax.ShapeDt...]
    gather x46 -> x0, local copies, waits for them, and re-layouts: 38.4 us -> none
    all_to_all x1 -> x0, blocking collectives: 19.4 us -> none  [shards(): lax.all_to_all(windows, 'chan', split_axis=0, concat_axis=0, tiled=True)]
    dot_general x3 -> x0, matrix products: 15 us -> none  [the longest x1 11.2 us: shards(): product = jnp.dot(stacked, traces, preferred_element_type=jnp.float32)]
    reshape x5 -> x0, local copies, waits for them, and re-layouts: 9.48 us -> none  [the longest x1 4.88 us: skew_sum(): return flattened.reshape(height, length + 1)[:, :count_out].sum(axis=0)]
    reduce_sum x4 -> x0, other arithmetic: 8.45 us -> none  [the longest x1 6.03 us: unit_masses(): squares.reshape(unit_count, unit_width, trace_rows.shape[1]).sum(axis=1)]
    another operation x1 -> x0, other arithmetic: 6.92 us -> none  [window_energy(): lax.reduce_window(segments, jnp.zeros((), segments.dtype), lax.add, (1, T...]
  transfers between devices with their start and end apart: 2 -> 0, of which waited for: 2 -> 0; matrix products, arithmetic and copies ran while one was open for 15% -> 0% of each run, Pallas kernels for 0% -> 0%
where the time goes in v1:
time: 64.6 us; the launch traced here: 64.3 us
  Pallas kernels  58.2 us (90%)
  local copies, waits for them, and re-layouts  6.13 us (9%)
    pallas_call x1, Pallas kernels, shards(): pl.pallas_call(functools.partial(kernel, ntm, nch), out_shape=jax.ShapeDt...  58.2 us
    unnamed x11, local copies, waits for them, and re-layouts  6.13 us

profile of v1, /device:TPU:0, one launch (start us, length us, event | category | flops | bytes accessed | tf_op | source)
XLA Modules:
  0.0 64.3 jit_solution(16660226048472633693)
XLA Ops:
  0.0 0.0 copy-start
  0.0 1.9 %copy-done = bf16[8,200,1024]{2,1,0:T(8,128)(2,1)S(1)} copy-done((bf16[8,200,1024]{2,1,0:T(8,128)(2,1)S(1)}, bf16[8,200,1024]{2,1,0:T(8,128)(2,1)}, u32[]{:S(2)}) %copy-start) | copy-done | bytes 3276824
  1.9 0.0 copy-start.1
  1.9 1.4 %copy-done.1 = f32[256,1408]{1,0:T(8,128)S(1)} copy-done((f32[256,1408]{1,0:T(8,128)S(1)}, f32[256,1408]{1,0:T(8,128)}, u32[]{:S(2)}) %copy-start.1) | copy-done | bytes 1441816
  3.3 0.0 copy-start.2
  3.3 0.9 %copy-done.2 = s32[8,4096]{1,0:T(8,128)S(1)} copy-done((s32[8,4096]{1,0:T(8,128)S(1)}, s32[8,4096]{1,0:T(8,128)}, u32[]{:S(2)}) %copy-start.2) | copy-done | bytes 131096
  4.2 0.0 copy-start.3
  4.2 0.7 %copy-done.3 = f32[129]{0:T(256)S(1)} copy-done((f32[129]{0:T(256)S(1)}, f32[129]{0:T(256)}, u32[]{:S(2)}) %copy-start.3) | copy-done | bytes 540
  4.9 0.0 copy-start.4
  4.9 0.7 %copy-done.4 = s32[8]{0:T(128)S(1)} copy-done((s32[8]{0:T(128)S(1)}, s32[8]{0:T(128)}, u32[]{:S(2)}) %copy-start.4) | copy-done | bytes 56
  5.5 58.2 %shard_map.55 = f32[8,256]{1,0:T(8,128)S(1)} custom-call(f32[256,1408]{1,0:T(8,128)S(1)} %copy-done.1, f32[1,129]{1,0:T(1,128)S(1)} %bitcast.1, bf16[8,200,1024]{2,1,0:T(8,128)(2,1)S(1)} %copy-done, s32[8,4096]{1,0:T(8,128)S(1)} %copy-done.2, s32[8]{0:T(128)S(1)} %copy-done.4), custom_call_target="tpu_custom_call" | custom-call | tf_op jit(solution)/shard_map/pallas_call | solution.py:288
  63.7 0.6 copy.7
Async XLA Ops:
  0.0 1.9 %copy-start = (bf16[8,200,1024]{2,1,0:T(8,128)(2,1)S(1)}, bf16[8,200,1024]{2,1,0:T(8,128)(2,1)}, u32[]{:S(2)}) copy-start(bf16[8,200,1024]{2,1,0:T(8,128)(2,1)} %tmpl_hbm.1) | copy-start | bytes 9830404
  1.9 1.4 %copy-start.1 = (f32[256,1408]{1,0:T(8,128)S(1)}, f32[256,1408]{1,0:T(8,128)}, u32[]{:S(2)}) copy-start(f32[256,1408]{1,0:T(8,128)} %raw_hbm.1) | copy-start | bytes 4325380
  3.3 0.9 %copy-start.2 = (s32[8,4096]{1,0:T(8,128)S(1)}, s32[8,4096]{1,0:T(8,128)}, u32[]{:S(2)}) copy-start(s32[8,4096]{1,0:T(8,128)} %mask_hbm.1) | copy-start | bytes 393220
  4.2 0.7 %copy-start.3 = (f32[129]{0:T(256)S(1)}, f32[129]{0:T(256)}, u32[]{:S(2)}) copy-start(f32[129]{0:T(256)} %param.6) | copy-start | bytes 1552
  4.9 0.7 %copy-start.4 = (s32[8]{0:T(128)S(1)}, s32[8]{0:T(128)}, u32[]{:S(2)}) copy-start(s32[8]{0:T(128)} %offs_ref.1) | copy-start | bytes 100

commit v2 on v1

--- a/solution.py
+++ b/solution.py
@@ -20,10 +20,10 @@
 
 
 def kernel(
-    ntm, nch, raw_hbm, taps_ref, tmpl_hbm, mask_hbm, offs_ref, out_ref,
+    ntm, nch, lend, raw_hbm, taps_ref, tmpl_hbm, mask_hbm, offs_ref, out_ref,
     raw, tap_row, tmpl, mask, skewed, shaped, rall, prod, qacc, units, num_out, en_out,
-    num_in, en_in, load_sem, recv_sem, right_sem, left_sem, unit_send, unit_recv,
-    num_send, num_recv, en_send, en_recv,
+    num_in, en_in, guest, gacc, gsum, load_sem, raw_sem, recv_sem, right_sem, left_sem,
+    unit_right, unit_left, unit_recv, num_send, num_recv, en_send, en_recv, guest_sem, gsum_sem,
 ):
     z = lax.axis_index("tmpl")
     c = lax.axis_index("chan")
@@ -34,21 +34,34 @@
     unit = min(LANE, rows)
     nun = rows // unit
 
+    def load_raw(n, first):
+        at = pl.ds(0, BLK + LANE) if first else pl.ds(pl.multiple_of(n * BLK + LANE, LANE), BLK)
+        return pltpu.make_async_copy(raw_hbm.at[:, at], raw.at[:, at], raw_sem.at[n])
+
+    for n in range(nblk):
+        load_raw(n, n == 0).start()
     loads = [
-        pltpu.make_async_copy(raw_hbm, raw, load_sem.at[0]),
-        pltpu.make_async_copy(tmpl_hbm, tmpl, load_sem.at[1]),
+        pltpu.make_async_copy(tmpl_hbm, tmpl, load_sem.at[0]),
         pltpu.make_async_copy(
-            mask_hbm.at[:, pl.ds(pl.multiple_of(c * local, LANE), local)], mask, load_sem.at[2]
+            mask_hbm.at[:, pl.ds(pl.multiple_of(c * local, LANE), local)], mask, load_sem.at[1]
         ),
     ]
     for item in loads:
         item.start()
 
     barrier = pltpu.get_barrier_semaphore()
-    for d in range(1, ntm):
+    @pl.when(z < ntm - 1)
+    def _():
         pl.semaphore_signal(
-            barrier, inc=1, device_id={"tmpl": lax.rem(z + d, ntm)}, device_id_type=MESH
-        )
+            barrier, inc=1, device_id={"tmpl": lax.rem(z + 1, ntm)}, device_id_type=MESH
+        )
+
+    @pl.when(z > 0)
+    def _():
+        pl.semaphore_signal(
+            barrier, inc=1, device_id={"tmpl": lax.rem(z - 1 + ntm, ntm)}, device_id_type=MESH
+        )
+
     for d in range(1, nch):
         pl.semaphore_signal(
             barrier, inc=1, device_id={"chan": lax.rem(c + d, nch)}, device_id_type=MESH
@@ -62,8 +75,21 @@
     band_hi = band.astype(jnp.bfloat16)
     band_lo = (band - band_hi.astype(jnp.float32)).astype(jnp.bfloat16)
     qacc[...] = jnp.zeros_like(qacc)
-    loads[0].wait()
-    pl.semaphore_wait(barrier, ntm - 1 + nch - 1)
+    is_end = (z == 0) | (z == ntm - 1)
+    is_helper = (z == 1) | (z == ntm - 2)
+    inward = jnp.where(z == 0, 1, ntm - 2)
+    outward = jnp.where(z == 1, 0, ntm - 1)
+    if lend:
+        @pl.when(is_end)
+        def _():
+            at = pl.ds(pl.multiple_of(inward * rows, rows), rows)
+            for n in range(nblk):
+                rall[n, at, :] = jnp.zeros((rows, BLK), jnp.bfloat16)
+
+    load_raw(0, True).wait()
+    pl.semaphore_wait(
+        barrier, jnp.where(z < ntm - 1, 1, 0) + jnp.where(z > 0, 1, 0) + (nch - 1)
+    )
 
     def chunk(src, n):
         return rall.at[n, pl.ds(pl.multiple_of(src * rows, rows), rows), :]
@@ -103,33 +129,44 @@
                     y[u * unit : (u + 1) * unit], axis=0, keepdims=True
                 )
 
-        @pl.when(z < ntm - 1)
+        @pl.when(z < ntm - 1 - lend)
         def _():
             hop(z, n, right_sem, 1).start()
 
-        @pl.when(z > 0)
+        @pl.when(z > lend)
         def _():
             hop(z, n, left_sem, -1).start()
 
         return carry
 
-    lax.fori_loop(0, nblk, fir, 0)
-
-    def unit_copy(src, d):
+    fir(0, 0)
+
+    def fir_next(n, carry):
+        load_raw(n, False).wait()
+        return fir(n, carry)
+
+    lax.fori_loop(1, nblk, fir_next, 0)
+
+    def unit_hop(src, sems, step):
         return pltpu.make_async_remote_copy(
             src_ref=units.at[src],
             dst_ref=units.at[src],
-            send_sem=unit_send.at[d],
-            recv_sem=unit_recv.at[d],
-            device_id={"tmpl": lax.rem(z + d, ntm)},
+            send_sem=sems.at[src],
+            recv_sem=unit_recv.at[src],
+            device_id={"tmpl": lax.rem(z + step + ntm, ntm)},
             device_id_type=MESH,
         )
 
-    for d in range(1, ntm):
-        unit_copy(z, d).start()
-
+    @pl.when(z < ntm - 1)
+    def _():
+        unit_hop(z, unit_right, 1).start()
+
+    @pl.when(z > 0)
+    def _():
+        unit_hop(z, unit_left, -1).start()
+
+    loads[0].wait()
     loads[1].wait()
-    loads[2].wait()
 
     def shape_cols(i, carry):
         cols = pl.ds(pl.multiple_of(i * LANE, LANE), LANE)
@@ -143,6 +180,32 @@
         return carry
 
     lax.fori_loop(0, local // LANE, shape_cols, 0)
+
+    def lend_copy(peer):
+        cols = pl.ds(pl.multiple_of(inward * rows, rows), rows)
+        return pltpu.make_async_remote_copy(
+            src_ref=shaped.at[:, cols],
+            dst_ref=guest,
+            send_sem=guest_sem.at[0],
+            recv_sem=guest_sem.at[1],
+            device_id={"tmpl": peer},
+            device_id_type=MESH,
+        )
+
+    def gsum_copy(peer):
+        return pltpu.make_async_remote_copy(
+            src_ref=gacc.at[:, pl.ds(BLK, total)],
+            dst_ref=gsum,
+            send_sem=gsum_sem.at[0],
+            recv_sem=gsum_sem.at[1],
+            device_id={"tmpl": peer},
+            device_id_type=MESH,
+        )
+
+    if lend:
+        @pl.when(is_end)
+        def _():
+            lend_copy(inward).start()
 
     offs = jnp.zeros((group, 1), jnp.int32)
     index = lax.broadcasted_iota(jnp.int32, (group, 1), 0)
@@ -187,7 +250,24 @@
         return value
 
     for d in range(1, ntm):
-        unit_copy(lax.rem(z + ntm - d, ntm), d).wait()
+        @pl.when(z - d >= 0)
+        def _():
+            src = lax.rem(z - d + ntm, ntm)
+            unit_hop(src, unit_right, 1).wait_recv()
+
+            @pl.when(z < ntm - 1)
+            def _():
+                unit_hop(src, unit_right, 1).start()
+
+        @pl.when(z + d < ntm)
+        def _():
+            src = lax.rem(z + d, ntm)
+            unit_hop(src, unit_left, -1).wait_recv()
+
+            @pl.when(z > 0)
+            def _():
+                unit_hop(src, unit_left, -1).start()
+
     masses = jnp.zeros((group, total), jnp.float32)
     for s in range(ntm):
         for u in range(nun):
@@ -205,7 +285,9 @@
     spread(shift_rows(energy), en_out, en_in, en_send, en_recv)
 
     def arrive(d, n):
-        @pl.when(z - d >= 0)
+        near = lend if d == 1 else 0
+
+        @pl.when((z - d >= 0) & (z < ntm - near))
         def _():
             src = lax.rem(z - d + ntm, ntm)
             hop(src, n, right_sem, 1).wait_recv()
@@ -214,7 +296,7 @@
             def _():
                 hop(src, n, right_sem, 1).start()
 
-        @pl.when(z + d < ntm)
+        @pl.when((z + d < ntm) & (z >= near))
         def _():
             src = lax.rem(z + d, ntm)
             hop(src, n, left_sem, -1).wait_recv()
@@ -223,9 +305,8 @@
             def _():
                 hop(src, n, left_sem, -1).start()
 
-    def block(n, carry):
-        arrive(ntm - 1, n)
-        prod[...] = jnp.dot(shaped[...], rall[n], preferred_element_type=jnp.float32)
+    def skew(n, weights, samples, acc):
+        prod[...] = jnp.dot(weights, samples, preferred_element_type=jnp.float32)
         blank = jnp.zeros((group, LANE), jnp.float32)
         total_acc = jnp.zeros((group, 2 * BLK), jnp.float32)
         for g in range(min(LANE, tlen)):
@@ -239,7 +320,16 @@
             wide = jnp.concatenate([blank, carry_in, first, second], axis=1)
             total_acc = total_acc + left(wide, g)
         at = pl.ds(pl.multiple_of(n * BLK, BLK), 2 * BLK)
-        qacc[:, at] = qacc[:, at] + total_acc
+        acc[:, at] = acc[:, at] + total_acc
+
+    def block(n, carry):
+        for d in range(max(1, ntm // 2), ntm):
+            arrive(d, n)
+        skew(n, shaped[...], rall[n], qacc)
+        return carry
+
+    def guest_block(n, carry):
+        skew(n, guest[...], chunk(z, n)[...], gacc)
         return carry
 
     def step(d):
@@ -249,9 +339,22 @@
 
         lax.fori_loop(0, nblk, body, 0)
 
-    for d in range(1, ntm - 1):
+    for d in range(1, max(1, ntm // 2)):
         step(d)
     lax.fori_loop(0, nblk, block, 0)
+
+    if lend:
+        @pl.when(is_helper)
+        def _():
+            gacc[...] = jnp.zeros_like(gacc)
+            lend_copy(outward).wait_recv()
+            lax.fori_loop(0, nblk, guest_block, 0)
+            gsum_copy(outward).start()
+
+        @pl.when(is_end)
+        def _():
+            gsum_copy(inward).wait_recv()
+            qacc[:, BLK:] = qacc[:, BLK:] + gsum[...]
 
     spread(shift_rows(qacc[:, BLK:]), num_out, num_in, num_send, num_recv)
     energy = collect(en_out, en_in, en_send, en_recv)
@@ -260,17 +363,34 @@
 
     def drain(n, carry):
         for s in range(ntm):
-            @pl.when((s <= z) & (z < ntm - 1))
+            @pl.when((s <= z) & (z < ntm - 1) & ((s != z) | (z < ntm - 1 - lend)))
             def _():
                 hop(s, n, right_sem, 1).wait_send()
 
-            @pl.when((s >= z) & (z > 0))
+            @pl.when((s >= z) & (z > 0) & ((s != z) | (z > lend)))
             def _():
                 hop(s, n, left_sem, -1).wait_send()
 
         return carry
 
     lax.fori_loop(0, nblk, drain, 0)
+    for s in range(ntm):
+        @pl.when((s <= z) & (z < ntm - 1))
+        def _():
+            unit_hop(s, unit_right, 1).wait_send()
+
+        @pl.when((s >= z) & (z > 0))
+        def _():
+            unit_hop(s, unit_left, -1).wait_send()
+
+    if lend:
+        @pl.when(is_end)
+        def _():
+            lend_copy(inward).wait_send()
+
+        @pl.when(is_helper)
+        def _():
+            gsum_copy(outward).wait_send()
 
 
 def shards(raw_traces, filter_taps, templates, offsets, channel_mask):
@@ -282,11 +402,12 @@
     total = nblk * BLK
     lag = (total - SPAN) // nch
     nun = rows // min(LANE, rows)
+    lend = int(ntm >= 4 and rows % LANE == 0)
     f32, bf16, dma = jnp.float32, jnp.bfloat16, pltpu.SemaphoreType.DMA
     any_spec = pl.BlockSpec(memory_space=pl.ANY)
     vmem_spec = pl.BlockSpec(memory_space=pltpu.VMEM)
     return pl.pallas_call(
-        functools.partial(kernel, ntm, nch),
+        functools.partial(kernel, ntm, nch, lend),
         out_shape=jax.ShapeDtypeStruct((group, lag), f32),
         in_specs=[
             any_spec, vmem_spec, any_spec, any_spec, pl.BlockSpec(memory_space=pltpu.SMEM),
@@ -307,19 +428,26 @@
             pltpu.VMEM((nch, group, lag), f32),
             pltpu.VMEM((nch, group, lag), f32),
             pltpu.VMEM((nch, group, lag), f32),
-            dma((3,)),
+            pltpu.VMEM((group * tlen, rows if lend else LANE), bf16),
+            pltpu.VMEM((group, BLK + total), f32),
+            pltpu.VMEM((group, total), f32),
+            dma((2,)),
+            dma((nblk,)),
             dma((ntm, nblk)),
             dma((ntm, nblk)),
             dma((ntm, nblk)),
+            dma((ntm,)),
             dma((ntm,)),
             dma((ntm,)),
             dma((nch,)),
             dma((nch,)),
             dma((nch,)),
             dma((nch,)),
+            dma((2,)),
+            dma((2,)),
         ],
         compiler_params=pltpu.CompilerParams(
-            collective_id=0, has_side_effects=True, vmem_limit_bytes=48 * 1024 * 1024
+            collective_id=0, has_side_effects=True, vmem_limit_bytes=60 * 1024 * 1024
         ),
     )(raw_traces, filter_taps.reshape(1, -1), templates, channel_mask, offsets)
 

time: 64.6 us -> 62.2 us (0.963)
  local copies, waits for them, and re-layouts: 6.13 us -> 1.3 us
  Pallas kernels: 58.2 us -> 60.7 us
    unnamed x11 -> x1, local copies, waits for them, and re-layouts: 6.13 us -> 1.3 us
    pallas_call x1, Pallas kernels: 58.2 us -> 60.7 us  [shards(): pl.pallas_call(functools.partial(kernel, ntm, nch, lend), out_shape=jax.S...]
where the time goes in v2:
time: 62.2 us; the launch traced here: 62 us
  Pallas kernels  60.7 us (98%)
  local copies, waits for them, and re-layouts  1.3 us (2%)
    pallas_call x1, Pallas kernels, shards(): pl.pallas_call(functools.partial(kernel, ntm, nch, lend), out_shape=jax.S...  60.7 us
    unnamed x1, local copies, waits for them, and re-layouts  1.3 us

profile of v2, /device:TPU:0, one launch (start us, length us, event | category | flops | bytes accessed | tf_op | source)
XLA Modules:
  0.0 62.0 jit_solution(16014253187703138570)
XLA Ops:
  0.0 60.7 %shard_map.55 = f32[8,256]{1,0:T(8,128)} custom-call(f32[256,1408]{1,0:T(8,128)} %raw_hbm.1, f32[1,129]{1,0:T(1,128)} %bitcast.1, bf16[8,200,1024]{2,1,0:T(8,128)(2,1)} %tmpl_hbm.1, s32[8,4096]{1,0:T(8,128)} %mask_hbm.1, s32[8]{0:T(128)} %offs_ref.1), custom_call_target="tpu_custom_call" | custom-call | tf_op jit(solution)/shard_map/pallas_call | solution.py:409
  60.7 1.3 %copy.7 = f32[8,256]{1,0:T(8,128)} copy(f32[8,256]{1,0:T(8,128)} %shard_map.55) | data formatting | bytes 16384

commit v3 on v2

--- a/solution.py
+++ b/solution.py
@@ -11,6 +11,7 @@
 BLK = 256
 LANE = 128
 MESH = pl.DeviceIdType.MESH
+PIECES = 2
 
 
 def left(x, count):
@@ -94,12 +95,14 @@
     def chunk(src, n):
         return rall.at[n, pl.ds(pl.multiple_of(src * rows, rows), rows), :]
 
-    def hop(src, n, sems, step):
+    def hop(src, n, h, sems, step):
+        height = rows // PIECES
+        at = pl.ds(pl.multiple_of(src * rows + h * height, height), height)
         return pltpu.make_async_remote_copy(
-            src_ref=chunk(src, n),
-            dst_ref=chunk(src, n),
-            send_sem=sems.at[src, n],
-            recv_sem=recv_sem.at[src, n],
+            src_ref=rall.at[n, at, :],
+            dst_ref=rall.at[n, at, :],
+            send_sem=sems.at[src, n * PIECES + h],
+            recv_sem=recv_sem.at[src, n * PIECES + h],
             device_id={"tmpl": lax.rem(z + step + ntm, ntm)},
             device_id_type=MESH,
         )
@@ -129,23 +132,24 @@
                     y[u * unit : (u + 1) * unit], axis=0, keepdims=True
                 )
 
+        return carry
+
+    def send_own(n, carry):
         @pl.when(z < ntm - 1 - lend)
         def _():
-            hop(z, n, right_sem, 1).start()
+            for h in range(PIECES):
+                hop(z, n, h, right_sem, 1).start()
 
         @pl.when(z > lend)
         def _():
-            hop(z, n, left_sem, -1).start()
-
-        return carry
-
-    fir(0, 0)
+            for h in range(PIECES):
+                hop(z, n, h, left_sem, -1).start()
+
+        return carry
 
     def fir_next(n, carry):
         load_raw(n, False).wait()
         return fir(n, carry)
-
-    lax.fori_loop(1, nblk, fir_next, 0)
 
     def unit_hop(src, sems, step):
         return pltpu.make_async_remote_copy(
@@ -157,6 +161,10 @@
             device_id_type=MESH,
         )
 
+    fir(0, 0)
+    send_own(0, 0)
+    lax.fori_loop(1, nblk, fir_next, 0)
+
     @pl.when(z < ntm - 1)
     def _():
         unit_hop(z, unit_right, 1).start()
@@ -164,6 +172,8 @@
     @pl.when(z > 0)
     def _():
         unit_hop(z, unit_left, -1).start()
+
+    lax.fori_loop(1, nblk, send_own, 0)
 
     loads[0].wait()
     loads[1].wait()
@@ -249,7 +259,7 @@
             value = value + in_ref[d]
         return value
 
-    for d in range(1, ntm):
+    def unit_arrive(d):
         @pl.when(z - d >= 0)
         def _():
             src = lax.rem(z - d + ntm, ntm)
@@ -268,21 +278,22 @@
             def _():
                 unit_hop(src, unit_left, -1).start()
 
-    masses = jnp.zeros((group, total), jnp.float32)
-    for s in range(ntm):
-        for u in range(nun):
-            at = s * rows + u * unit
-            flag = mask[:, at : at + 1].astype(jnp.float32)
-            masses = masses + flag * units[s, u : u + 1, :]
-    window, width, place, energy = masses, 1, 0, None
-    while width <= tlen:
-        if tlen & width:
-            piece = left(window, place)
-            energy = piece if energy is None else energy + piece
-            place += width
-        window = window + left(window, width)
-        width *= 2
-    spread(shift_rows(energy), en_out, en_in, en_send, en_recv)
+    def send_energy():
+        masses = jnp.zeros((group, total), jnp.float32)
+        for s in range(ntm):
+            for u in range(nun):
+                at = s * rows + u * unit
+                flag = mask[:, at : at + 1].astype(jnp.float32)
+                masses = masses + flag * units[s, u : u + 1, :]
+        window, width, place, energy = masses, 1, 0, None
+        while width <= tlen:
+            if tlen & width:
+                piece = left(window, place)
+                energy = piece if energy is None else energy + piece
+                place += width
+            window = window + left(window, width)
+            width *= 2
+        spread(shift_rows(energy), en_out, en_in, en_send, en_recv)
 
     def arrive(d, n):
         near = lend if d == 1 else 0
@@ -290,20 +301,22 @@
         @pl.when((z - d >= 0) & (z < ntm - near))
         def _():
             src = lax.rem(z - d + ntm, ntm)
-            hop(src, n, right_sem, 1).wait_recv()
-
-            @pl.when(z < ntm - 1)
-            def _():
-                hop(src, n, right_sem, 1).start()
+            for h in range(PIECES):
+                hop(src, n, h, right_sem, 1).wait_recv()
+
+                @pl.when(z < ntm - 1)
+                def _():
+                    hop(src, n, h, right_sem, 1).start()
 
         @pl.when((z + d < ntm) & (z >= near))
         def _():
             src = lax.rem(z + d, ntm)
-            hop(src, n, left_sem, -1).wait_recv()
-
-            @pl.when(z > 0)
-            def _():
-                hop(src, n, left_sem, -1).start()
+            for h in range(PIECES):
+                hop(src, n, h, left_sem, -1).wait_recv()
+
+                @pl.when(z > 0)
+                def _():
+                    hop(src, n, h, left_sem, -1).start()
 
     def skew(n, weights, samples, acc):
         prod[...] = jnp.dot(weights, samples, preferred_element_type=jnp.float32)
@@ -325,6 +338,13 @@
     def block(n, carry):
         for d in range(max(1, ntm // 2), ntm):
             arrive(d, n)
+
+        @pl.when(n == min(1, nblk - 1))
+        def _():
+            for d in range(max(1, ntm // 2), ntm):
+                unit_arrive(d)
+            send_energy()
+
         skew(n, shaped[...], rall[n], qacc)
         return carry
 
@@ -335,6 +355,11 @@
     def step(d):
         def body(n, carry):
             arrive(d, n)
+
+            @pl.when(n == 0)
+            def _():
+                unit_arrive(d)
+
             return carry
 
         lax.fori_loop(0, nblk, body, 0)
@@ -365,11 +390,13 @@
         for s in range(ntm):
             @pl.when((s <= z) & (z < ntm - 1) & ((s != z) | (z < ntm - 1 - lend)))
             def _():
-                hop(s, n, right_sem, 1).wait_send()
+                for h in range(PIECES):
+                    hop(s, n, h, right_sem, 1).wait_send()
 
             @pl.when((s >= z) & (z > 0) & ((s != z) | (z > lend)))
             def _():
-                hop(s, n, left_sem, -1).wait_send()
+                for h in range(PIECES):
+                    hop(s, n, h, left_sem, -1).wait_send()
 
         return carry
 
@@ -433,9 +460,9 @@
             pltpu.VMEM((group, total), f32),
             dma((2,)),
             dma((nblk,)),
-            dma((ntm, nblk)),
-            dma((ntm, nblk)),
-            dma((ntm, nblk)),
+            dma((ntm, nblk * PIECES)),
+            dma((ntm, nblk * PIECES)),
+            dma((ntm, nblk * PIECES)),
             dma((ntm,)),
             dma((ntm,)),
             dma((ntm,)),

time: 62.2 us -> 51.6 us (0.83)
  Pallas kernels: 60.7 us -> 50 us
    pallas_call x1, Pallas kernels: 60.7 us -> 50 us  [shards(): pl.pallas_call(functools.partial(kernel, ntm, nch, lend), out_shape=jax.S...]
where the time goes in v3:
time: 51.6 us; the launch traced here: 51.3 us
  Pallas kernels  50 us (97%)
  local copies, waits for them, and re-layouts  1.3 us (3%)
    pallas_call x1, Pallas kernels, shards(): pl.pallas_call(functools.partial(kernel, ntm, nch, lend), out_shape=jax.S...  50 us
    unnamed x1, local copies, waits for them, and re-layouts  1.3 us

profile of v3, /device:TPU:0, one launch (start us, length us, event | category | flops | bytes accessed | tf_op | source)
XLA Modules:
  0.0 51.3 jit_solution(7836428797559887248)
XLA Ops:
  0.0 50.0 %shard_map.55 = f32[8,256]{1,0:T(8,128)} custom-call(f32[256,1408]{1,0:T(8,128)} %raw_hbm.1, f32[1,129]{1,0:T(1,128)} %bitcast.1, bf16[8,200,1024]{2,1,0:T(8,128)(2,1)} %tmpl_hbm.1, s32[8,4096]{1,0:T(8,128)} %mask_hbm.1, s32[8]{0:T(128)} %offs_ref.1), custom_call_target="tpu_custom_call" | custom-call | tf_op jit(solution)/shard_map/pallas_call | solution.py:436
  50.0 1.3 %copy.7 = f32[8,256]{1,0:T(8,128)} copy(f32[8,256]{1,0:T(8,128)} %shard_map.55) | data formatting | bytes 16384

commit v4 on v3

--- a/solution.py
+++ b/solution.py
@@ -11,7 +11,7 @@
 BLK = 256
 LANE = 128
 MESH = pl.DeviceIdType.MESH
-PIECES = 2
+PIECES = 1
 
 
 def left(x, count):
@@ -21,8 +21,8 @@
 
 
 def kernel(
-    ntm, nch, lend, raw_hbm, taps_ref, tmpl_hbm, mask_hbm, offs_ref, out_ref,
-    raw, tap_row, tmpl, mask, skewed, shaped, rall, prod, qacc, units, num_out, en_out,
+    ntm, nch, lend, raw_hbm, taps_hbm, tmpl_hbm, mask_hbm, offs_hbm, out_ref,
+    taps_ref, offs_ref, raw, tap_row, tmpl, mask, skewed, shaped, rall, prod, qacc, units, num_out, en_out,
     num_in, en_in, guest, gacc, gsum, load_sem, raw_sem, recv_sem, right_sem, left_sem,
     unit_right, unit_left, unit_recv, num_send, num_recv, en_send, en_recv, guest_sem, gsum_sem,
 ):
@@ -39,6 +39,8 @@
         at = pl.ds(0, BLK + LANE) if first else pl.ds(pl.multiple_of(n * BLK + LANE, LANE), BLK)
         return pltpu.make_async_copy(raw_hbm.at[:, at], raw.at[:, at], raw_sem.at[n])
 
+    load_taps = pltpu.make_async_copy(taps_hbm, taps_ref, load_sem.at[2])
+    load_taps.start()
     for n in range(nblk):
         load_raw(n, n == 0).start()
     loads = [
@@ -46,6 +48,7 @@
         pltpu.make_async_copy(
             mask_hbm.at[:, pl.ds(pl.multiple_of(c * local, LANE), local)], mask, load_sem.at[1]
         ),
+        pltpu.make_async_copy(offs_hbm, offs_ref, load_sem.at[3]),
     ]
     for item in loads:
         item.start()
@@ -69,6 +72,7 @@
         )
 
     tap_row[...] = jnp.zeros_like(tap_row)
+    load_taps.wait()
     tap_row[:, : taps_ref.shape[1]] = taps_ref[...]
     band = pltpu.roll(
         jnp.broadcast_to(tap_row[...], (LANE, 2 * LANE)), 0, 1, stride=1, stride_axis=0
@@ -88,9 +92,6 @@
                 rall[n, at, :] = jnp.zeros((rows, BLK), jnp.bfloat16)
 
     load_raw(0, True).wait()
-    pl.semaphore_wait(
-        barrier, jnp.where(z < ntm - 1, 1, 0) + jnp.where(z > 0, 1, 0) + (nch - 1)
-    )
 
     def chunk(src, n):
         return rall.at[n, pl.ds(pl.multiple_of(src * rows, rows), rows), :]
@@ -162,6 +163,9 @@
         )
 
     fir(0, 0)
+    pl.semaphore_wait(
+        barrier, jnp.where(z < ntm - 1, 1, 0) + jnp.where(z > 0, 1, 0) + (nch - 1)
+    )
     send_own(0, 0)
     lax.fori_loop(1, nblk, fir_next, 0)
 
@@ -175,8 +179,8 @@
 
     lax.fori_loop(1, nblk, send_own, 0)
 
-    loads[0].wait()
-    loads[1].wait()
+    for item in loads:
+        item.wait()
 
     def shape_cols(i, carry):
         cols = pl.ds(pl.multiple_of(i * LANE, LANE), LANE)
@@ -191,13 +195,17 @@
 
     lax.fori_loop(0, local // LANE, shape_cols, 0)
 
-    def lend_copy(peer):
+    cut = min(LANE, tlen) * group
+    parts = [(0, cut), (cut, tlen * group - cut)]
+
+    def lend_copy(p, peer):
         cols = pl.ds(pl.multiple_of(inward * rows, rows), rows)
+        lines = pl.ds(*parts[p])
         return pltpu.make_async_remote_copy(
-            src_ref=shaped.at[:, cols],
-            dst_ref=guest,
-            send_sem=guest_sem.at[0],
-            recv_sem=guest_sem.at[1],
+            src_ref=shaped.at[lines, cols],
+            dst_ref=guest.at[lines, :],
+            send_sem=guest_sem.at[0, p],
+            recv_sem=guest_sem.at[1, p],
             device_id={"tmpl": peer},
             device_id_type=MESH,
         )
@@ -215,7 +223,8 @@
     if lend:
         @pl.when(is_end)
         def _():
-            lend_copy(inward).start()
+            lend_copy(0, inward).start()
+            lend_copy(1, inward).start()
 
     offs = jnp.zeros((group, 1), jnp.int32)
     index = lax.broadcasted_iota(jnp.int32, (group, 1), 0)
@@ -318,23 +327,40 @@
                 def _():
                     hop(src, n, h, left_sem, -1).start()
 
-    def skew(n, weights, samples, acc):
-        prod[...] = jnp.dot(weights, samples, preferred_element_type=jnp.float32)
+    def skew(n, weights, samples, acc, begin, end):
+        prod[: weights.shape[0], :] = jnp.dot(
+            weights, samples, preferred_element_type=jnp.float32
+        )
         blank = jnp.zeros((group, LANE), jnp.float32)
         total_acc = jnp.zeros((group, 2 * BLK), jnp.float32)
+
+        def row(tap):
+            if tap < begin or tap >= end:
+                return None
+            line = (tap - begin) * group
+            return prod[line : line + group, :]
+
         for g in range(min(LANE, tlen)):
-            low = prod[group * g : group * (g + 1), :]
-            first, second = low[:, :LANE], low[:, LANE:]
-            carry_in = blank
-            if g + LANE < tlen:
-                high = prod[group * (g + LANE) : group * (g + LANE + 1), :]
+            low, high = row(g), row(g + LANE)
+            if low is None and high is None:
+                continue
+            carry_in, first, second = blank, blank, blank
+            if low is not None:
+                first, second = low[:, :LANE], low[:, LANE:]
+            if high is not None:
                 carry_in = high[:, :LANE]
-                first = first + high[:, LANE:]
+                first = high[:, LANE:] if low is None else first + high[:, LANE:]
             wide = jnp.concatenate([blank, carry_in, first, second], axis=1)
             total_acc = total_acc + left(wide, g)
         at = pl.ds(pl.multiple_of(n * BLK, BLK), 2 * BLK)
         acc[:, at] = acc[:, at] + total_acc
 
+    def guest_block(p, n, carry):
+        line, count = parts[p]
+        weights = guest[line : line + count, :]
+        skew(n, weights, chunk(z, n)[...], gacc, line // group, (line + count) // group)
+        return carry
+
     def block(n, carry):
         for d in range(max(1, ntm // 2), ntm):
             arrive(d, n)
@@ -345,11 +371,14 @@
                 unit_arrive(d)
             send_energy()
 
-        skew(n, shaped[...], rall[n], qacc)
-        return carry
-
-    def guest_block(n, carry):
-        skew(n, guest[...], chunk(z, n)[...], gacc)
+        if lend:
+            @pl.when((n == nblk - 1) & is_helper)
+            def _():
+                gacc[...] = jnp.zeros_like(gacc)
+                lend_copy(0, outward).wait_recv()
+                lax.fori_loop(0, nblk, functools.partial(guest_block, 0), 0)
+
+        skew(n, shaped[...], rall[n], qacc, 0, tlen)
         return carry
 
     def step(d):
@@ -371,9 +400,8 @@
     if lend:
         @pl.when(is_helper)
         def _():
-            gacc[...] = jnp.zeros_like(gacc)
-            lend_copy(outward).wait_recv()
-            lax.fori_loop(0, nblk, guest_block, 0)
+            lend_copy(1, outward).wait_recv()
+            lax.fori_loop(0, nblk, functools.partial(guest_block, 1), 0)
             gsum_copy(outward).start()
 
         @pl.when(is_end)
@@ -413,7 +441,8 @@
     if lend:
         @pl.when(is_end)
         def _():
-            lend_copy(inward).wait_send()
+            lend_copy(0, inward).wait_send()
+            lend_copy(1, inward).wait_send()
 
         @pl.when(is_helper)
         def _():
@@ -429,7 +458,7 @@
     total = nblk * BLK
     lag = (total - SPAN) // nch
     nun = rows // min(LANE, rows)
-    lend = int(ntm >= 4 and rows % LANE == 0)
+    lend = int(ntm >= 4 and rows % LANE == 0 and tlen > LANE)
     f32, bf16, dma = jnp.float32, jnp.bfloat16, pltpu.SemaphoreType.DMA
     any_spec = pl.BlockSpec(memory_space=pl.ANY)
     vmem_spec = pl.BlockSpec(memory_space=pltpu.VMEM)
@@ -437,10 +466,12 @@
         functools.partial(kernel, ntm, nch, lend),
         out_shape=jax.ShapeDtypeStruct((group, lag), f32),
         in_specs=[
-            any_spec, vmem_spec, any_spec, any_spec, pl.BlockSpec(memory_space=pltpu.SMEM),
+            any_spec, any_spec, any_spec, any_spec, any_spec,
         ],
         out_specs=vmem_spec,
         scratch_shapes=[
+            pltpu.VMEM((1, filter_taps.shape[0]), f32),
+            pltpu.SMEM((group,), jnp.int32),
             pltpu.VMEM((rows, length), f32),
             pltpu.VMEM((1, 2 * LANE), f32),
             pltpu.VMEM((group, tlen, local), bf16),
@@ -458,7 +489,7 @@
             pltpu.VMEM((group * tlen, rows if lend else LANE), bf16),
             pltpu.VMEM((group, BLK + total), f32),
             pltpu.VMEM((group, total), f32),
-            dma((2,)),
+            dma((4,)),
             dma((nblk,)),
             dma((ntm, nblk * PIECES)),
             dma((ntm, nblk * PIECES)),
@@ -470,7 +501,7 @@
             dma((nch,)),
             dma((nch,)),
             dma((nch,)),
-            dma((2,)),
+            dma((2, 2)),
             dma((2,)),
         ],
         compiler_params=pltpu.CompilerParams(

time: 51.6 us -> 50 us (0.969)
  Pallas kernels: 50 us -> 48.5 us
    pallas_call x1, Pallas kernels: 50 us -> 48.5 us  [shards(): pl.pallas_call(functools.partial(kernel, ntm, nch, lend), out_shape=jax.S...]
where the time goes in v4:
time: 50 us; the launch traced here: 49.8 us
  Pallas kernels  48.5 us (97%)
  local copies, waits for them, and re-layouts  1.3 us (3%)
    pallas_call x1, Pallas kernels, shards(): pl.pallas_call(functools.partial(kernel, ntm, nch, lend), out_shape=jax.S...  48.5 us
    unnamed x1, local copies, waits for them, and re-layouts  1.3 us

profile of v4, /device:TPU:0, one launch (start us, length us, event | category | flops | bytes accessed | tf_op | source)
XLA Modules:
  0.0 49.8 jit_solution(17558636247473901384)
XLA Ops:
  0.0 48.5 %shard_map.55 = f32[8,256]{1,0:T(8,128)} custom-call(f32[256,1408]{1,0:T(8,128)} %raw_hbm.1, f32[1,129]{1,0:T(1,128)} %bitcast.1, bf16[8,200,1024]{2,1,0:T(8,128)(2,1)} %tmpl_hbm.1, s32[8,4096]{1,0:T(8,128)} %mask_hbm.1, s32[8]{0:T(128)} %offs_hbm.1), custom_call_target="tpu_custom_call" | custom-call | tf_op jit(solution)/shard_map/pallas_call | solution.py:465
  48.5 1.3 %copy.7 = f32[8,256]{1,0:T(8,128)} copy(f32[8,256]{1,0:T(8,128)} %shard_map.55) | data formatting | bytes 16384
